TPU v7x, 128 devices: a whole 4x4x4 slice. The times are simulated.
128 devices in a mesh: req: 16 (over z, y), mlp: 8 (over x, core).
Axes of the slice: x: 4, y: 4, z: 4, core: 2. Of those that a mesh axis runs over, the one named last changes fastest.
Arguments:
- tokens: bfloat16 [4096, 2048], P('req', 'mlp'), may hold values from -5 to 5
- attn_gain: float32 [2048], replicated, may hold values from 0.5 to 1.5
- mlp_gain: float32 [2048], replicated, may hold values from 0.5 to 1.5
- final_gain: float32 [2048], replicated, may hold values from 0.25 to 4
- q_gain: float32 [64], replicated, may hold values from 0.5 to 1.5
- k_gain: float32 [64], replicated, may hold values from 0.25 to 4
- w_query: bfloat16 [2048, 2048], P(None, 'mlp'), may hold values from -0.125 to 0.125
- w_keyval: bfloat16 [2048, 1024], P(None, 'mlp'), may hold values from -0.125 to 0.125
- w_out: bfloat16 [2048, 2048], P('mlp'), may hold values from -0.125 to 0.125
- w_gate: bfloat16 [2048, 8192], P(None, 'mlp'), may hold values from -0.125 to 0.125
- w_up: bfloat16 [2048, 8192], P(None, 'mlp'), may hold values from -0.125 to 0.125
- w_down: bfloat16 [8192, 2048], P('mlp'), may hold values from -0.0625 to 0.0625
- w_head: bfloat16 [2048, 65536], P('req', 'mlp'), may hold values from -0.42 to 0.42
- targets: int32 [4096], P('req'), may hold values from 0 to 65535
- req_lengths: int32 [16, 4], P('req'), may hold values from 1 to 128, 256 in all within a row
- req_tenant: int32 [16, 4], P('req'), may hold values from 0 to 3
- prefix_piece: int32 [16], replicated, may hold values from 0 to 15, each once
- prefix_kv: bfloat16 [16, 1024, 1024], P('req', None, 'mlp'), may hold values from -160 to 160
Outputs:
- hidden_out: bfloat16 [4096, 2048], P('req', 'mlp')
- logprob: float32 [4096], P('req')
Inputs may be any that keep to these rules, and one draw needn't show every extreme that they name: `req_lengths`: each row sums to 256; its longest request has exactly 128 tokens. `prefix_piece`: every piece number appears once; piece n is part n % 4 of the prefix of tenant n // 4.
All inputs are finite; a program needn't handle non-finite values.
Results may differ from a plain program's by a relative error of at most 0.023.
Values may be sent and summed in bfloat16 or wider, within the bound.
A program may use at most 128 MiB of HBM per device.

v0:
```python
import math
import jax
import jax.numpy as jnp
from jax import lax
from jax.sharding import PartitionSpec as P

TENANTS = 4
PLEN = 4096
EPS = 1e-05
LOG_THETA = math.log(1000000.0)
NEG = -1e30


def rms_norm(values, gain):
    return values * lax.rsqrt(jnp.mean(values * values, axis=-1, keepdims=True) + EPS) * gain


def rope_tables(position, size):
    half = size // 2
    freq = jnp.exp(jnp.arange(half, dtype=jnp.float32) * (-2.0 * LOG_THETA / size))
    angle = position[:, None] * freq[None, :]
    return (jnp.cos(angle), jnp.sin(angle))


def rotate(values, cosine, sine):
    half = values.shape[-1] // 2
    first = values[..., :half]
    second = values[..., half:]
    cosine = cosine[:, None, :]
    sine = sine[:, None, :]
    return jnp.concatenate(
        [first * cosine - second * sine, first * sine + second * cosine], axis=-1
    )


def row_layout(lengths, tenants, count):
    ends = jnp.cumsum(lengths)
    row_ids = jnp.arange(count, dtype=jnp.int32)
    request = jnp.sum((row_ids[:, None] >= ends[None, :]).astype(jnp.int32), axis=1)
    onehot = (request[:, None] == jnp.arange(lengths.shape[0], dtype=jnp.int32)[None, :]).astype(
        jnp.int32
    )
    starts = ends - lengths
    offset = row_ids - jnp.sum(onehot * starts[None, :], axis=1)
    tenant = jnp.sum(onehot * tenants[None, :], axis=1)
    return (request, offset, tenant)


def absorb(state, queries, keys, values, seen, scale):
    best, total, accum = state
    scores = jnp.einsum("kqd,knd->kqn", queries, keys, preferred_element_type=jnp.float32) * scale
    scores = jnp.where(seen[None], scores, NEG)
    new_best = jnp.maximum(best, jnp.max(scores, axis=-1))
    keep = jnp.exp(best - new_best)
    weights = jnp.where(seen[None], jnp.exp(scores - new_best[..., None]), 0.0)
    total = total * keep + jnp.sum(weights, axis=-1)
    accum = accum * keep[..., None] + jnp.einsum(
        "kqn,knd->kqd", weights.astype(jnp.bfloat16), values, preferred_element_type=jnp.float32
    )
    return (new_best, total, accum)


def body(
    tokens,
    attn_gain,
    mlp_gain,
    final_gain,
    q_gain,
    k_gain,
    w_query,
    w_keyval,
    w_out,
    w_gate,
    w_up,
    w_down,
    w_head,
    targets,
    req_lengths,
    req_tenant,
    prefix_piece,
    prefix_kv,
):
    rows = tokens.shape[0]
    head_size = q_gain.shape[0]
    local_kv = w_keyval.shape[1] // (2 * head_size)
    local_q = w_query.shape[1] // head_size
    group = local_q // local_kv
    split_count = lax.axis_size("req") // TENANTS
    scale = head_size ** (-0.5)
    stream = lax.all_gather(tokens, "mlp", axis=1, tiled=True)
    stream_f = stream.astype(jnp.float32)
    normed = rms_norm(stream_f, attn_gain).astype(jnp.bfloat16)
    query = jnp.dot(normed, w_query, preferred_element_type=jnp.float32).reshape(
        rows, local_q, head_size
    )
    keyval = jnp.dot(normed, w_keyval, preferred_element_type=jnp.float32).reshape(
        rows, local_kv, 2, head_size
    )
    request, offset, tenant = row_layout(req_lengths[0], req_tenant[0], rows)
    cosine, sine = rope_tables((PLEN + offset).astype(jnp.float32), head_size)
    query = rotate(rms_norm(query, q_gain), cosine, sine).astype(jnp.bfloat16)
    own_keys = (
        rotate(rms_norm(keyval[:, :, 0], k_gain), cosine, sine)
        .astype(jnp.bfloat16)
        .transpose(1, 0, 2)
    )
    own_vals = keyval[:, :, 1].astype(jnp.bfloat16).transpose(1, 0, 2)
    queries = (
        query.reshape(rows, local_kv, group, head_size)
        .transpose(1, 2, 0, 3)
        .reshape(local_kv, group * rows, head_size)
    )
    start_state = (
        jnp.full((local_kv, group * rows), NEG, jnp.float32),
        jnp.zeros((local_kv, group * rows), jnp.float32),
        jnp.zeros((local_kv, group * rows, head_size), jnp.float32),
    )
    piece = lax.all_gather(prefix_kv, "req", axis=0, tiled=True)
    slab = piece.shape[1]

    def one_piece(index, inner_state):
        block = lax.dynamic_index_in_dim(piece, index, 0, keepdims=False).reshape(
            slab, local_kv, 2, head_size
        )
        block_keys = block[:, :, 0].transpose(1, 0, 2)
        block_vals = block[:, :, 1].transpose(1, 0, 2)
        owner_tenant = (
            lax.dynamic_index_in_dim(prefix_piece, index, 0, keepdims=False) // split_count
        )
        seen = jnp.tile(tenant == owner_tenant, group)[:, None]
        return absorb(inner_state, queries, block_keys, block_vals, seen, scale)

    state = lax.fori_loop(0, piece.shape[0], one_piece, start_state)
    row_ids = jnp.arange(rows, dtype=jnp.int32)
    causal = (request[:, None] == request[None, :]) & (row_ids[None, :] <= row_ids[:, None])
    best, total, accum = absorb(
        state, queries, own_keys, own_vals, jnp.tile(causal, (group, 1)), scale
    )
    attended = (
        (accum / total[..., None])
        .reshape(local_kv, group, rows, head_size)
        .transpose(2, 0, 1, 3)
        .reshape(rows, local_q * head_size)
        .astype(jnp.bfloat16)
    )
    attn_proj = jnp.dot(attended, w_out, preferred_element_type=jnp.float32)
    attn_part = lax.psum_scatter(
        attn_proj.astype(jnp.bfloat16), "mlp", scatter_dimension=1, tiled=True
    ).astype(jnp.float32)
    mid_share = (tokens.astype(jnp.float32) + attn_part).astype(jnp.bfloat16)
    middle = lax.all_gather(mid_share, "mlp", axis=1, tiled=True)
    middle_f = middle.astype(jnp.float32)
    normed_mid = rms_norm(middle_f, mlp_gain).astype(jnp.bfloat16)
    gate = jnp.dot(normed_mid, w_gate, preferred_element_type=jnp.float32)
    upper = jnp.dot(normed_mid, w_up, preferred_element_type=jnp.float32)
    inner = (jax.nn.silu(gate) * upper).astype(jnp.bfloat16)
    down = jnp.dot(inner, w_down, preferred_element_type=jnp.float32)
    down_part = lax.psum_scatter(
        down.astype(jnp.bfloat16), "mlp", scatter_dimension=1, tiled=True
    ).astype(jnp.float32)
    out_share = (mid_share.astype(jnp.float32) + down_part).astype(jnp.bfloat16)
    hidden_full = lax.all_gather(out_share, "mlp", axis=1, tiled=True)
    normed_out = rms_norm(hidden_full.astype(jnp.float32), final_gain).astype(jnp.bfloat16)
    vocab_local = w_head.shape[1]
    logits = jnp.dot(
        normed_out,
        lax.all_gather(w_head, "req", axis=0, tiled=True),
        preferred_element_type=jnp.float32,
    )
    vocab_start = lax.axis_index("mlp") * vocab_local
    top = lax.pmax(jnp.max(logits, axis=1), "mlp")
    hit = targets[:, None] - vocab_start == jnp.arange(vocab_local, dtype=jnp.int32)[None, :]
    totals, picked = lax.psum(
        (
            jnp.sum(jnp.exp(logits - top[:, None]), axis=1),
            jnp.sum(jnp.where(hit, logits, 0.0), axis=1),
        ),
        "mlp",
    )
    logprob = picked - top - jnp.log(totals)
    return (out_share, logprob)


def solution(mesh):
    in_specs = (
        P("req", "mlp"),
        P(),
        P(),
        P(),
        P(),
        P(),
        P(None, "mlp"),
        P(None, "mlp"),
        P("mlp", None),
        P(None, "mlp"),
        P(None, "mlp"),
        P("mlp", None),
        P("req", "mlp"),
        P("req"),
        P("req", None),
        P("req", None),
        P(),
        P("req", None, "mlp"),
    )
    out_specs = (P("req", "mlp"), P("req"))
    return jax.shard_map(body, mesh=mesh, in_specs=in_specs, out_specs=out_specs, check_vma=False)
```

profile of v0, /device:TPU:1, one launch (start us, length us, event | category | flops | bytes accessed | tf_op | source)
XLA Modules:
  0.0 688.8 jit_solution(6187407375356977096)
XLA Ops:
  11.8 24.9 %all-gather.8.cloned.1.call-done = bf16[256,2048]{1,0:T(8,128)(2,1)} async-done(((bf16[256,256]{1,0:T(8,128)(2,1)}), bf16[256,2048]{1,0:T(8,128)(2,1)}) %all-gather.8.cloned.1.call-update) | async-done | bytes 1048592 | tf_op jit(solution)/shard_map/all_gather | solution.py:90
  43.5 47.6 %all-gather.6.cloned.1.call-done = bf16[16,1024,128]{2,1,0:T(8,128)(2,1)} async-done(((bf16[1,1024,128]{2,1,0:T(8,128)(2,1)}), bf16[16,1024,128]{2,1,0:T(8,128)(2,1)}) %all-gather.6.cloned.1.call-update) | async-done | bytes 4194320 | tf_op jit(solution)/shard_map/all_gather | solution.py:118
  91.1 210.3 %while.20 = (s32[]{:T(128)}, f32[1,1024]{1,0:T(1,128)S(1)}, f32[1,1024]{1,0:T(1,128)S(1)}, f32[1,1024,64]{1,2,0:T(8,128)}, s32[16]{0:T(128)S(1)}, /*index=5*/s32...) while((s32[]{:T(128)}, f32[1,1024]{1,0:T(1,128)S(1)}, ...), condition=%wide.region_9.10_spmd.clone, body=%wide.region_6.0_spmd.clone.sunk | while | flops 282268928 | bytes 31530828 | solution.py:133
  95.5 2.7 fusion.94
  98.2 3.3 fusion.96
  107.7 2.7 fusion.94
  110.5 3.3 fusion.96
  120.9 2.7 fusion.94
  123.7 3.3 fusion.96
  127.1 2.7 fusion.98
  134.1 2.7 fusion.94
  136.9 3.3 fusion.96
  147.4 2.7 fusion.94
  150.1 3.3 fusion.96
  153.5 2.7 fusion.98
  160.6 2.7 fusion.94
  163.3 3.3 fusion.96
  173.8 2.7 fusion.94
  176.5 3.3 fusion.96
  187.0 2.7 fusion.94
  189.7 3.3 fusion.96
  200.2 2.7 fusion.94
  202.9 3.3 fusion.96
  213.4 2.7 fusion.94
  216.1 3.3 fusion.96
  226.6 2.7 fusion.94
  229.3 3.3 fusion.96
  239.8 2.7 fusion.94
  242.5 3.3 fusion.96
  253.0 2.7 fusion.94
  255.7 3.3 fusion.96
  266.2 2.7 fusion.94
  268.9 3.3 fusion.96
  279.4 2.7 fusion.94
  282.1 3.3 fusion.96
  292.6 2.7 fusion.94
  295.3 3.3 fusion.96
  304.6 28.8 %reduce-scatter.3.cloned.1.call-done = bf16[256,256]{1,0:T(8,128)(2,1)} async-done(((bf16[256,2048]{1,0:T(8,128)(2,1)}), bf16[256,256]{1,0:T(8,128)(2,1)}) %reduce-scatter.3.cloned.1.call-update) | async-done | bytes 131088 | tf_op jit(solution)/shard_map/reduce_scatter | solution.py:147
  335.0 25.8 %all-gather.10.cloned.1.call-done = bf16[256,2048]{1,0:T(8,128)(2,1)} async-done(((bf16[256,256]{1,0:T(8,128)(2,1)}), bf16[256,2048]{1,0:T(8,128)(2,1)}) %all-gather.10.cloned.1.call-update) | async-done | bytes 1048592 | tf_op jit(solution)/shard_map/all_gather | solution.py:151
  362.5 4.8 fusion.46
  367.3 7.3 %convolution_convert_fusion = bf16[256,2048]{1,0:T(8,128)(2,1)} fusion(bf16[1024,2048]{1,0:T(8,128)(2,1)} %param.31, bf16[2048,1024]{1,0:T(8,128)(2,1)} %param.30, f32[256,1024]{1,0:T(8,128)} %fusion.46, bf16[256,2048]{1,0:T(8,128)(2,1)S(1)} %copy-done.5, f32[2048]{0:T(1024)S(1)} %copy-done.11, f32[256]{0:T(256)S(1)} %add_rsqrt_fusion.2), kind=kOutput, calls=%fused_computation.34 | convolution fusion | flops 2151677952 | bytes 11543552 | tf_op jit(solution)/shard_map/dot_general | solution.py:157
  374.7 29.8 %reduce-scatter.5.cloned.1.call-done = bf16[256,256]{1,0:T(8,128)(2,1)} async-done(((bf16[256,2048]{1,0:T(8,128)(2,1)}), bf16[256,256]{1,0:T(8,128)(2,1)}) %reduce-scatter.5.cloned.1.call-update) | async-done | bytes 131088 | tf_op jit(solution)/shard_map/reduce_scatter | solution.py:158
  406.9 25.1 %all-gather.12.cloned.1.call-done = bf16[256,2048]{1,0:T(8,128)(2,1)} async-done(((bf16[256,256]{1,0:T(8,128)(2,1)}), bf16[256,2048]{1,0:T(8,128)(2,1)}) %all-gather.12.cloned.1.call-update) | async-done | bytes 1048592 | tf_op jit(solution)/shard_map/all_gather | solution.py:162
  433.5 198.5 %all-gather.14.cloned.1.call-done = bf16[2048,8192]{1,0:T(8,128)(2,1)} async-done(((bf16[128,8192]{1,0:T(8,128)(2,1)}), bf16[2048,8192]{1,0:T(8,128)(2,1)}) %all-gather.14.cloned.1.call-update) | async-done | bytes 33554448 | tf_op jit(solution)/shard_map/all_gather | solution.py:167
  632.0 17.4 %fusion.77 = (f32[256]{0:T(256)S(1)}, f32[256,8192]{1,0:T(8,128)}) fusion(bf16[2048,8192]{1,0:T(8,128)(2,1)} %all-gather.14.cloned.1.call-done, bf16[256,2048]{1,0:T(8,128)(2,1)} %all-gather.12.cloned.1.call-done, f32[2048]{0:T(1024)S(1)} %copy-done.12, f32[256]{0:T(256)S(1)} %add_rsqrt_fusion.1), kind=kOutput, calls=%fused_computation.123 | convolution fusion | flops 8594128896 | bytes 43001856 | tf_op jit(solution)/shard_map/dot_general | solution.py:165
  649.3 12.4 %pmax.7 = f32[256]{0:T(256)S(1)} all-reduce(f32[256]{0:T(256)S(1)} %get-tuple-element.289), channel_id=1, replica_groups=mesh['req'=16,'mlp'=8] {'mlp'}, use_global_device_ids=true, to_apply=%region_20.21 | all-reduce | flops 256 | bytes 2048 | tf_op jit(solution)/shard_map/pmax | solution.py:171
  661.8 5.1 select_reduce_fusion
  666.9 14.5 %all-reduce = (f32[256]{0:T(256)S(1)}, f32[256]{0:T(256)S(1)}) all-reduce(f32[256]{0:T(256)S(1)} %get-tuple-element.250, f32[256]{0:T(256)S(1)} %get-tuple-element.249), channel_id=1, replica_groups=mesh['req'=16,'mlp'=8] {'mlp'}, use_global_device_ids=true, to_apply=%region_22.23 | all-reduce | flops 512 | bytes 4096 | tf_op jit(solution)/shard_map/psum | solution.py:173
  (272 shorter events, 88.3 us)
Async XLA Ops:
  7.2 295.9 %copy-start = (bf16[256,2048]{1,0:T(8,128)(2,1)S(1)}, bf16[256,2048]{1,0:T(8,128)(2,1)}, u32[]{:S(2)}) copy-start(bf16[256,2048]{1,0:T(8,128)(2,1)} %param.28) | copy-start | bytes 3145732
  7.2 34.0 %copy-start.10 = (f32[2048]{0:T(1024)S(1)}, f32[2048]{0:T(1024)}, u32[]{:S(2)}) copy-start(f32[2048]{0:T(1024)} %param.21) | copy-start | bytes 24580
  7.2 33.4 %copy-start.8 = (f32[64]{0:T(128)S(1)}, f32[64]{0:T(128)}, u32[]{:S(2)}) copy-start(f32[64]{0:T(128)} %param.24) | copy-start | bytes 772
  7.2 29.5 %all-gather.8.cloned.1.call-start = ((), (), s32[]{:S(2)}) async-start(), calls=%async_computation.3 | async-start | bytes 1179648 | tf_op jit(solution)/shard_map/all_gather | solution.py:90
  7.9 83.2 %all-gather.6.cloned.1.call-start = ((), (), s32[]{:S(2)}) async-start(), calls=%async_computation.2 | async-start | bytes 4456448 | tf_op jit(solution)/shard_map/all_gather | solution.py:118
  8.7 324.7 %reduce-scatter.3.cloned.1.call-start = ((), (), s32[]{:S(2)}) async-start(), calls=%async_computation.4 | async-start | bytes 1179648 | tf_op jit(solution)/shard_map/reduce_scatter | solution.py:147
  11.8 31.1 %copy-start.9 = (f32[64]{0:T(128)S(1)}, f32[64]{0:T(128)}, u32[]{:S(2)}) copy-start(f32[64]{0:T(128)} %param.25) | copy-start | bytes 772
  36.7 4.5 copy-start.4
  38.3 52.8 %copy-start.13 = (s32[16]{0:T(128)S(1)}, s32[16]{0:T(128)}, u32[]{:S(2)}) copy-start(s32[16]{0:T(128)} %param.36) | copy-start | bytes 196
  98.2 3.4 copy-start.2
  110.5 3.4 copy-start.2
  123.7 3.4 copy-start.2
  136.9 3.4 copy-start.2
  150.1 3.4 copy-start.2
  163.3 3.4 copy-start.2
  176.5 3.4 copy-start.2
  189.7 3.4 copy-start.2
  202.9 3.4 copy-start.2
  216.1 3.4 copy-start.2
  229.3 3.4 copy-start.2
  242.5 3.4 copy-start.2
  255.7 3.4 copy-start.2
  268.9 3.4 copy-start.2
  282.1 3.4 copy-start.2
  295.3 3.4 copy-start.2
  301.4 31.9 %copy-start.6 = (bf16[256,256]{1,0:T(8,128)(2,1)S(1)}, bf16[256,256]{1,0:T(8,128)(2,1)}, u32[]{:S(2)}) copy-start(bf16[256,256]{1,0:T(8,128)(2,1)} %param.20) | copy-start | bytes 393220
  301.7 60.8 %copy-start.11 = (f32[2048]{0:T(1024)S(1)}, f32[2048]{0:T(1024)}, u32[]{:S(2)}) copy-start(f32[2048]{0:T(1024)} %param.22) | copy-start | bytes 24580
  304.6 56.3 %all-gather.10.cloned.1.call-start = ((), (), s32[]{:S(2)}) async-start(), calls=%async_computation.5 | async-start | bytes 1179648 | tf_op jit(solution)/shard_map/all_gather | solution.py:151
  335.0 69.5 %reduce-scatter.5.cloned.1.call-start = ((), (), s32[]{:S(2)}) async-start(), calls=%async_computation.6 | async-start | bytes 1179648 | tf_op jit(solution)/shard_map/reduce_scatter | solution.py:158
  360.9 6.4 copy-start.5
  367.3 37.2 %copy-start.3 = (bf16[256,256]{1,0:T(8,128)(2,1)S(1)}, bf16[256,256]{1,0:T(8,128)(2,1)}, u32[]{:S(2)}) copy-start(bf16[256,256]{1,0:T(8,128)(2,1)} %add_convert_fusion.1) | copy-start | bytes 393220
  367.3 39.6 %copy-start.7 = (s32[256]{0:T(256)S(1)}, s32[256]{0:T(256)}, u32[]{:S(2)}) copy-start(s32[256]{0:T(256)} %param.33) | copy-start | bytes 3076
  374.6 257.3 %copy-start.12 = (f32[2048]{0:T(1024)S(1)}, f32[2048]{0:T(1024)}, u32[]{:S(2)}) copy-start(f32[2048]{0:T(1024)} %param.23) | copy-start | bytes 24580
  374.7 57.3 %all-gather.12.cloned.1.call-start = ((), (), s32[]{:S(2)}) async-start(), calls=%async_computation.7 | async-start | bytes 1179648 | tf_op jit(solution)/shard_map/all_gather | solution.py:162
  406.1 225.8 %all-gather.14.cloned.1.call-start = ((), (), s32[]{:S(2)}) async-start(), calls=%async_computation.8 | async-start | bytes 35651584 | tf_op jit(solution)/shard_map/all_gather | solution.py:167
  661.8 20.2 %copy-start.1 = (bf16[256,2048]{1,0:T(8,128)(2,1)S(1)}, bf16[256,2048]{1,0:T(8,128)(2,1)}, u32[]{:S(2)}) copy-start(bf16[256,2048]{1,0:T(8,128)(2,1)} %param.28) | copy-start | bytes 3145732
Sparse Core Ops, SparseCore 0:
  9.7 26.9 all-gather.7
  38.8 52.2 all-gather.5
  304.7 28.6 reduce-scatter.2
  335.5 25.3 all-gather.9
  374.8 29.6 reduce-scatter.4
  406.6 25.3 all-gather.11
  434.1 197.7 all-gather.13
where the time goes:
time: 691 us; the launch traced here: 689 us
  waiting for transfers between devices  382 us (55%)
  matrix products  122 us (18%)
  other arithmetic  70.8 us (10%)
  loops' own time  42.2 us (6%)
  local copies, waits for them, and re-layouts  29.7 us (4%)
  blocking collectives  27 us (4%)
  between operations  14.4 us (2%)
    all_gather x1, waiting for transfers between devices, body(): lax.all_gather(w_head, 'req', axis=0, tiled=True)  198 us
    reduce_sum x17, other arithmetic, absorb(): total = total * keep + jnp.sum(weights, axis=-1)  53.3 us
    all_gather x1, waiting for transfers between devices, body(): piece = lax.all_gather(prefix_kv, 'req', axis=0, tiled=True)  47.6 us
    dot_general x17, matrix products, absorb(): jnp.einsum('kqd,knd->kqn', queries, keys, preferred_element_type=jnp.floa...  43.9 us
    dot_general x17, matrix products, absorb(): jnp.einsum('kqn,knd->kqd', weights.astype(jnp.bfloat16), values, preferre...  43.1 us
    another operation x1, loops' own time, body(): state = lax.fori_loop(0, piece.shape[0], one_piece, start_state)  42.2 us
    reduce_scatter x1, waiting for transfers between devices, body(): lax.psum_scatter(down.astype(jnp.bfloat16), 'mlp', scatter_dimension=1, t...  29.8 us
    reduce_scatter x1, waiting for transfers between devices, body(): lax.psum_scatter(attn_proj.astype(jnp.bfloat16), 'mlp', scatter_dimension...  28.8 us
  transfers between devices with their start and end apart: 7, of which 7 were waited for; matrix products, arithmetic and copies ran while one was open for 2% of the time, Pallas kernels for 0%

commit v1 on v0

--- a/solution.py
+++ b/solution.py
@@ -87,7 +87,12 @@
     group = local_q // local_kv
     split_count = lax.axis_size("req") // TENANTS
     scale = head_size ** (-0.5)
-    stream = lax.all_gather(tokens, "mlp", axis=1, tiled=True)
+    ring = [tokens]
+    for hop in range(7):
+        ring.append(lax.ppermute(ring[-1], "mlp", [(dev, (dev + 1) % 8) for dev in range(8)]))
+    stream = jnp.roll(
+        jnp.concatenate(ring[::-1], axis=1), (lax.axis_index("mlp") + 1) * ring[0].shape[1], axis=1
+    )
     stream_f = stream.astype(jnp.float32)
     normed = rms_norm(stream_f, attn_gain).astype(jnp.bfloat16)
     query = jnp.dot(normed, w_query, preferred_element_type=jnp.float32).reshape(

time: 691 us -> 664 us (0.961)
  waiting for transfers between devices: 382 us -> 347 us
  starting transfers between devices: 0.46 us -> 11.2 us
    all_gather x1, waiting for transfers between devices: 47.6 us -> 15.2 us  [body(): piece = lax.all_gather(prefix_kv, 'req', axis=0, tiled=True)]
    all_gather x1 -> x0, waiting for transfers between devices: 24.9 us -> none  [body(): stream = lax.all_gather(tokens, 'mlp', axis=1, tiled=True)]
    ppermute x0 -> x7, waiting for transfers between devices: none -> 22.2 us  [body(): lax.ppermute(ring[-1], 'mlp', [(dev, (dev + 1) % 8) for dev in range(8)])]
    ppermute x0 -> x7, starting transfers between devices: none -> 10.8 us  [body(): lax.ppermute(ring[-1], 'mlp', [(dev, (dev + 1) % 8) for dev in range(8)])]
  transfers between devices with their start and end apart: 7 -> 13, of which waited for: 7 -> 13; matrix products, arithmetic and copies ran while one was open for 2% -> 1% of each run, Pallas kernels for 0% -> 0%
where the time goes in v1:
time: 664 us; the launch traced here: 662 us
  waiting for transfers between devices  347 us (52%)
  matrix products  119 us (18%)
  other arithmetic  69.4 us (10%)
  loops' own time  42.2 us (6%)
  local copies, waits for them, and re-layouts  31.3 us (5%)
  blocking collectives  27 us (4%)
  between operations  14.6 us (2%)
  starting transfers between devices  11.2 us (2%)
    all_gather x1, waiting for transfers between devices, body(): lax.all_gather(w_head, 'req', axis=0, tiled=True)  198 us
    reduce_sum x17, other arithmetic, absorb(): total = total * keep + jnp.sum(weights, axis=-1)  53.3 us
    dot_general x17, matrix products, absorb(): jnp.einsum('kqd,knd->kqn', queries, keys, preferred_element_type=jnp.floa...  44 us
    dot_general x17, matrix products, absorb(): jnp.einsum('kqn,knd->kqd', weights.astype(jnp.bfloat16), values, preferre...  43.1 us
    another operation x1, loops' own time, body(): state = lax.fori_loop(0, piece.shape[0], one_piece, start_state)  42.2 us
    reduce_scatter x1, waiting for transfers between devices, body(): lax.psum_scatter(down.astype(jnp.bfloat16), 'mlp', scatter_dimension=1, t...  29.8 us
    reduce_scatter x1, waiting for transfers between devices, body(): lax.psum_scatter(attn_proj.astype(jnp.bfloat16), 'mlp', scatter_dimension...  28.7 us
    all_gather x1, waiting for transfers between devices, body(): middle = lax.all_gather(mid_share, 'mlp', axis=1, tiled=True)  26 us
  transfers between devices with their start and end apart: 13, of which 13 were waited for; matrix products, arithmetic and copies ran while one was open for 1% of the time, Pallas kernels for 0%

profile of v1, /device:TPU:1, one launch (start us, length us, event | category | flops | bytes accessed | tf_op | source)
XLA Modules:
  0.0 661.7 jit_solution(12123885351366112311)
XLA Ops:
  24.1 3.2 collective-permute-done.3
  29.8 3.1 collective-permute-done.4
  33.3 5.2 collective-permute-done.5
  38.7 5.4 collective-permute-done.6
  49.9 15.2 %all-gather.5.cloned.1.call-done = bf16[16,1024,128]{2,1,0:T(8,128)(2,1)} async-done(((bf16[1,1024,128]{2,1,0:T(8,128)(2,1)}), bf16[16,1024,128]{2,1,0:T(8,128)(2,1)}) %all-gather.5.cloned.1.call-update) | async-done | bytes 4194320 | tf_op jit(solution)/shard_map/all_gather | solution.py:123
  65.1 210.5 %while.20 = (s32[]{:T(128)}, f32[1,1024]{1,0:T(1,128)S(1)}, f32[1,1024]{1,0:T(1,128)S(1)}, f32[1,1024,64]{1,2,0:T(8,128)}, s32[16]{0:T(128)S(1)}, /*index=5*/s32...) while((s32[]{:T(128)}, f32[1,1024]{1,0:T(1,128)S(1)}, ...), condition=%wide.region_9.10_spmd.clone, body=%wide.region_6.9_spmd.clone.sunk | while | flops 282268928 | bytes 31530828 | solution.py:138
  69.4 2.7 fusion.96
  72.2 3.3 fusion.98
  81.7 2.7 fusion.96
  84.4 3.3 fusion.98
  94.9 2.7 fusion.96
  97.7 3.3 fusion.98
  108.1 2.7 fusion.96
  110.9 3.3 fusion.98
  121.3 2.7 fusion.96
  124.1 3.3 fusion.98
  134.6 2.7 fusion.96
  137.3 3.3 fusion.98
  147.8 2.7 fusion.96
  150.5 3.3 fusion.98
  161.0 2.7 fusion.96
  163.7 3.3 fusion.98
  174.2 2.7 fusion.96
  176.9 3.3 fusion.98
  187.4 2.7 fusion.96
  190.1 3.3 fusion.98
  200.6 2.7 fusion.96
  203.4 3.3 fusion.98
  213.8 2.7 fusion.96
  216.6 3.3 fusion.98
  227.0 2.7 fusion.96
  229.8 3.3 fusion.98
  240.3 2.7 fusion.96
  243.0 3.3 fusion.98
  253.5 2.7 fusion.96
  256.2 3.3 fusion.98
  269.4 3.3 fusion.98
  278.7 28.7 %reduce-scatter.3.cloned.1.call-done = bf16[256,256]{1,0:T(8,128)(2,1)} async-done(((bf16[256,2048]{1,0:T(8,128)(2,1)}), bf16[256,256]{1,0:T(8,128)(2,1)}) %reduce-scatter.3.cloned.1.call-update) | async-done | bytes 131088 | tf_op jit(solution)/shard_map/reduce_scatter | solution.py:152
  309.1 26.0 %all-gather.7.cloned.1.call-done = bf16[256,2048]{1,0:T(8,128)(2,1)} async-done(((bf16[256,256]{1,0:T(8,128)(2,1)}), bf16[256,2048]{1,0:T(8,128)(2,1)}) %all-gather.7.cloned.1.call-update) | async-done | bytes 1048592 | tf_op jit(solution)/shard_map/all_gather | solution.py:156
  336.6 3.9 fusion.46
  340.6 7.1 %convolution_convert_fusion = bf16[256,2048]{1,0:T(8,128)(2,1)} fusion(bf16[1024,2048]{1,0:T(8,128)(2,1)} %param.31, bf16[2048,1024]{1,0:T(8,128)(2,1)} %param.30, f32[256,1024]{1,0:T(8,128)S(1)} %fusion.46, bf16[256,2048]{1,0:T(8,128)(2,1)S(1)} %copy-done.5, f32[2048]{0:T(1024)S(1)} %copy-done.13, f32[256]{0:T(256)S(1)} %add_rsqrt_fusion.2), kind=kOutput, calls=%fused_computation.34 | convolution fusion | flops 2151677952 | bytes 11543552 | tf_op jit(solution)/shard_map/dot_general | solution.py:162
  347.7 29.8 %reduce-scatter.5.cloned.1.call-done = bf16[256,256]{1,0:T(8,128)(2,1)} async-done(((bf16[256,2048]{1,0:T(8,128)(2,1)}), bf16[256,256]{1,0:T(8,128)(2,1)}) %reduce-scatter.5.cloned.1.call-update) | async-done | bytes 131088 | tf_op jit(solution)/shard_map/reduce_scatter | solution.py:163
  379.7 25.2 %all-gather.9.cloned.1.call-done = bf16[256,2048]{1,0:T(8,128)(2,1)} async-done(((bf16[256,256]{1,0:T(8,128)(2,1)}), bf16[256,2048]{1,0:T(8,128)(2,1)}) %all-gather.9.cloned.1.call-update) | async-done | bytes 1048592 | tf_op jit(solution)/shard_map/all_gather | solution.py:167
  406.5 198.3 %all-gather.11.cloned.1.call-done = bf16[2048,8192]{1,0:T(8,128)(2,1)} async-done(((bf16[128,8192]{1,0:T(8,128)(2,1)}), bf16[2048,8192]{1,0:T(8,128)(2,1)}) %all-gather.11.cloned.1.call-update) | async-done | bytes 33554448 | tf_op jit(solution)/shard_map/all_gather | solution.py:172
  604.8 17.4 %fusion.79 = (f32[256]{0:T(256)S(1)}, f32[256,8192]{1,0:T(8,128)}) fusion(bf16[2048,8192]{1,0:T(8,128)(2,1)} %all-gather.11.cloned.1.call-done, bf16[256,2048]{1,0:T(8,128)(2,1)} %all-gather.9.cloned.1.call-done, f32[2048]{0:T(1024)S(1)} %copy-done.14, f32[256]{0:T(256)S(1)} %add_rsqrt_fusion.1), kind=kOutput, calls=%fused_computation.141 | convolution fusion | flops 8594128896 | bytes 43001856 | tf_op jit(solution)/shard_map/dot_general | solution.py:170
  622.2 12.4 %pmax.7 = f32[256]{0:T(256)S(1)} all-reduce(f32[256]{0:T(256)S(1)} %get-tuple-element.289), channel_id=1, replica_groups=mesh['req'=16,'mlp'=8] {'mlp'}, use_global_device_ids=true, to_apply=%region_20.21 | all-reduce | flops 256 | bytes 2048 | tf_op jit(solution)/shard_map/pmax | solution.py:176
  634.6 5.1 select_reduce_fusion
  639.7 14.5 %all-reduce = (f32[256]{0:T(256)S(1)}, f32[256]{0:T(256)S(1)}) all-reduce(f32[256]{0:T(256)S(1)} %get-tuple-element.250, f32[256]{0:T(256)S(1)} %get-tuple-element.249), channel_id=1, replica_groups=mesh['req'=16,'mlp'=8] {'mlp'}, use_global_device_ids=true, to_apply=%region_22.23 | all-reduce | flops 512 | bytes 4096 | tf_op jit(solution)/shard_map/psum | solution.py:178
  (303 shorter events, 110.5 us)
Async XLA Ops:
  7.2 270.0 %copy-start = (bf16[256,2048]{1,0:T(8,128)(2,1)S(1)}, bf16[256,2048]{1,0:T(8,128)(2,1)}, u32[]{:S(2)}) copy-start(bf16[256,2048]{1,0:T(8,128)(2,1)} %param.28) | copy-start | bytes 3145732
  7.2 37.1 %copy-start.4 = (bf16[256,256]{1,0:T(8,128)(2,1)S(1)}, bf16[256,256]{1,0:T(8,128)(2,1)}, u32[]{:S(2)}) copy-start(bf16[256,256]{1,0:T(8,128)(2,1)} %param.20) | copy-start | bytes 393220
  7.2 57.9 %all-gather.5.cloned.1.call-start = ((), (), s32[]{:S(2)}) async-start(), calls=%async_computation.2 | async-start | bytes 4456448 | tf_op jit(solution)/shard_map/all_gather | solution.py:123
  7.9 299.5 %reduce-scatter.3.cloned.1.call-start = ((), (), s32[]{:S(2)}) async-start(), calls=%async_computation.3 | async-start | bytes 1179648 | tf_op jit(solution)/shard_map/reduce_scatter | solution.py:152
  8.0 4.9 collective-permute-start
  12.8 4.3 collective-permute-start.1
  17.1 4.5 collective-permute-start.2
  21.7 5.6 collective-permute-start.3
  27.3 5.6 collective-permute-start.4
  32.9 5.6 collective-permute-start.5
  38.5 5.6 collective-permute-start.6
  44.2 1.8 copy-start.10
  44.2 1.8 copy-start.12
  44.4 2.5 copy-start.6
  44.4 2.3 copy-start.8
  46.0 1.4 copy-start.11
  46.7 2.5 copy-start.9
  47.4 17.7 %copy-start.15 = (s32[16]{0:T(128)S(1)}, s32[16]{0:T(128)}, u32[]{:S(2)}) copy-start(s32[16]{0:T(128)} %param.36) | copy-start | bytes 196
  72.2 3.4 copy-start.2
  84.4 3.4 copy-start.2
  97.6 3.4 copy-start.2
  110.9 3.4 copy-start.2
  124.1 3.4 copy-start.2
  137.3 3.4 copy-start.2
  150.5 3.4 copy-start.2
  163.7 3.4 copy-start.2
  176.9 3.4 copy-start.2
  190.1 3.4 copy-start.2
  203.3 3.4 copy-start.2
  216.6 3.4 copy-start.2
  229.8 3.4 copy-start.2
  243.0 3.4 copy-start.2
  256.2 3.4 copy-start.2
  269.4 3.4 copy-start.2
  277.2 59.5 %copy-start.13 = (f32[2048]{0:T(1024)S(1)}, f32[2048]{0:T(1024)}, u32[]{:S(2)}) copy-start(f32[2048]{0:T(1024)} %param.22) | copy-start | bytes 24580
  278.6 56.5 %all-gather.7.cloned.1.call-start = ((), (), s32[]{:S(2)}) async-start(), calls=%async_computation.4 | async-start | bytes 1179648 | tf_op jit(solution)/shard_map/all_gather | solution.py:156
  309.1 68.4 %reduce-scatter.5.cloned.1.call-start = ((), (), s32[]{:S(2)}) async-start(), calls=%async_computation.5 | async-start | bytes 1179648 | tf_op jit(solution)/shard_map/reduce_scatter | solution.py:163
  336.6 3.9 copy-start.5
  340.5 37.0 %copy-start.3 = (bf16[256,256]{1,0:T(8,128)(2,1)S(1)}, bf16[256,256]{1,0:T(8,128)(2,1)}, u32[]{:S(2)}) copy-start(bf16[256,256]{1,0:T(8,128)(2,1)} %add_convert_fusion.1) | copy-start | bytes 393220
  347.6 32.1 %copy-start.7 = (s32[256]{0:T(256)S(1)}, s32[256]{0:T(256)}, u32[]{:S(2)}) copy-start(s32[256]{0:T(256)} %param.33) | copy-start | bytes 3076
  347.7 257.1 %copy-start.14 = (f32[2048]{0:T(1024)S(1)}, f32[2048]{0:T(1024)}, u32[]{:S(2)}) copy-start(f32[2048]{0:T(1024)} %param.23) | copy-start | bytes 24580
  347.7 57.3 %all-gather.9.cloned.1.call-start = ((), (), s32[]{:S(2)}) async-start(), calls=%async_computation.6 | async-start | bytes 1179648 | tf_op jit(solution)/shard_map/all_gather | solution.py:167
  379.1 225.7 %all-gather.11.cloned.1.call-start = ((), (), s32[]{:S(2)}) async-start(), calls=%async_computation.7 | async-start | bytes 35651584 | tf_op jit(solution)/shard_map/all_gather | solution.py:172
  634.6 20.2 %copy-start.1 = (bf16[256,2048]{1,0:T(8,128)(2,1)S(1)}, bf16[256,2048]{1,0:T(8,128)(2,1)}, u32[]{:S(2)}) copy-start(bf16[256,2048]{1,0:T(8,128)(2,1)} %param.28) | copy-start | bytes 3145732
Sparse Core Ops, SparseCore 0:
  10.2 54.8 all-gather.4
  278.8 28.6 reduce-scatter.2
  309.7 25.3 all-gather.6
  347.8 29.6 reduce-scatter.4
  379.6 25.3 all-gather.8
  407.0 197.7 all-gather.10
